TPU v7x, 256 devices: a whole 4x4x8 slice. The times are simulated.
256 devices in a mesh: span: 16 (over z, x_hi), sp: 8 (over y, x_lo), fsdp: 2 (over core).
Axes of the slice: x: 4 (x_hi: 2, x_lo: 2; x = x_hi * 2 + x_lo), y: 4, z: 8, core: 2. Of those that a mesh axis runs over, the one named last changes fastest.
Arguments:
- query_pre: bfloat16 [2, 16384, 3072], P('fsdp', ('span', 'sp')), may hold values from -12 to 12
- key_pre: bfloat16 [2, 16384, 3072], P('fsdp', ('span', 'sp')), may hold values from -12 to 12
- values: bfloat16 [2, 16384, 3072], P('fsdp', ('span', 'sp')), may hold values from -6 to 6
- cotangent: bfloat16 [2, 16384, 3072], P('fsdp', ('span', 'sp')), may hold values from -6 to 6
- gains: float32 [2, 3072], P(None, 'fsdp'), may hold values from 0.5 to 1.5
- frame_span: int32 [2, 16384], P('fsdp', 'span'), may hold values from 0 to 31, as said below
- denoise_steps: int32 [2, 32], P('fsdp'), may hold values from 1 to 4
Outputs:
- query_grad: bfloat16 [2, 16384, 3072], P('fsdp', ('span', 'sp'))
- key_grad: bfloat16 [2, 16384, 3072], P('fsdp', ('span', 'sp'))
- value_grad: bfloat16 [2, 16384, 3072], P('fsdp', ('span', 'sp'))
- gain_grad: float32 [2, 3072], P(None, 'fsdp')
Inputs may be any that keep to these rules, and one draw needn't show every extreme that they name: `frame_span`: never falls along a video. Group g (tokens g * 1024 to (g + 1) * 1024 - 1) holds frame spans 2 g and 2 g + 1, each from a quarter to three quarters of the group's tokens.
All inputs are finite; a program needn't handle non-finite values.
Results may differ from a plain program's by a relative error of at most 0.0081.
The roundings to bfloat16 on the way count: a program that leaves them out, or rounds other values in their place, can miss the bound.
Values may be sent and summed in bfloat16 or wider, within the bound.
No kernel may reach another device: no remote copies, remote signals or barrier semaphores. Data moves between devices by JAX's collectives and lax.ppermute only.
A program may use at most 128 MiB of HBM per device.

v0:
```python
import jax
import jax.numpy as jnp
from jax import lax
from jax.sharding import PartitionSpec as P

HDIM = 128
EPSILON = 1e-06
NEGATIVE = -1e30


def from_behind(value, axis, steps):
    count = lax.axis_size(axis)
    first, last = (max(0, -steps), min(count, count - steps))
    return lax.ppermute(value, axis, [(source, source + steps) for source in range(first, last)])


def normed(raw_rows, gain_row):
    wide = raw_rows.astype(jnp.float32)
    inverse_rms = lax.rsqrt(jnp.mean(wide * wide, axis=-1, keepdims=True) + EPSILON)
    normal_rows = wide * inverse_rms
    return (normal_rows, inverse_rms, (normal_rows * gain_row).astype(jnp.bfloat16))


def norm_backward(grad_rows, normal_rows, inverse_rms, gain_row):
    upstream = grad_rows.astype(jnp.float32)
    scaled = upstream * gain_row
    inner = jnp.mean(scaled * normal_rows, axis=-1, keepdims=True)
    result = (inverse_rms * (scaled - normal_rows * inner)).astype(jnp.bfloat16)
    return (result, jnp.sum(upstream * normal_rows, axis=0))


def across(left, right):
    return lax.dot_general(
        left, right, (((1,), (1,)), ((), ())), preferred_element_type=jnp.float32
    )


def downward(left, right):
    return lax.dot_general(
        left, right, (((0,), (0,)), ((), ())), preferred_element_type=jnp.float32
    )


def head_grads(
    query_head, grad_head, key_joined, value_joined, joined_mask, step_weight, own_width
):
    score_scale = HDIM ** (-0.5)
    scores = across(query_head, key_joined) * score_scale
    masked = jnp.where(joined_mask, scores, NEGATIVE)
    row_max = jnp.max(masked, axis=1)
    row_total = jnp.sum(jnp.exp(masked - row_max[:, None]), axis=1)
    log_total = row_max + jnp.log(row_total)
    grad_prob = across(grad_head, value_joined)
    probs = jnp.where(joined_mask, jnp.exp(scores - log_total[:, None]), 0.0)
    row_delta = jnp.sum(probs * grad_prob, axis=1)
    factor = step_weight[:, None]
    sgrad = (factor * probs * (grad_prob - row_delta[:, None])).astype(jnp.bfloat16)
    weights = (factor * probs).astype(jnp.bfloat16)
    query_part = jnp.dot(sgrad, key_joined, preferred_element_type=jnp.float32) * score_scale
    key_own_grad = downward(sgrad[:, :own_width], query_head) * score_scale
    value_own_grad = downward(weights[:, :own_width], grad_head)
    return (
        query_part,
        key_own_grad,
        value_own_grad,
        sgrad[:, own_width:],
        weights[:, own_width:],
        log_total,
        row_delta,
    )


def on_device(query_pre, key_pre, values, cotangent, gains, frame_span, denoise_steps):
    gain_full = lax.all_gather(gains, "fsdp", axis=1, tiled=True)
    q_normal, q_inverse, q_ready = normed(query_pre[0], gain_full[0])
    k_normal, k_inverse, k_ready = normed(key_pre[0], gain_full[1])
    heads_query, heads_key, heads_value, heads_grad = (
        lax.all_to_all(q_ready, "sp", split_axis=1, concat_axis=0, tiled=True),
        lax.all_to_all(k_ready, "sp", split_axis=1, concat_axis=0, tiled=True),
        lax.all_to_all(values[0], "sp", split_axis=1, concat_axis=0, tiled=True),
        lax.all_to_all(cotangent[0], "sp", split_axis=1, concat_axis=0, tiled=True),
    )
    head_count = heads_query.shape[1] // HDIM
    own_width = heads_query.shape[0]
    span_ids = frame_span[0]
    step_table = denoise_steps[0].astype(jnp.float32)
    matches = span_ids[:, None] == lax.iota(jnp.int32, step_table.shape[0])[None, :]
    step_weight = jnp.sum(jnp.where(matches, step_table[None, :], 0.0), axis=1)
    group_index = lax.axis_index("span")
    key_prev, value_prev = from_behind((heads_key, heads_value), "span", 1)
    own_mask = span_ids[None, :] <= span_ids[:, None]
    prev_open = group_index > 0
    prev_mask = jnp.broadcast_to(prev_open, own_mask.shape)
    joined_mask = jnp.concatenate([own_mask, prev_mask], axis=1)
    key_joined_all = jnp.concatenate([heads_key, key_prev], axis=0)
    value_joined_all = jnp.concatenate([heads_value, value_prev], axis=0)
    query_parts = []
    key_parts = []
    value_parts = []
    sgrad_list = []
    weight_list = []
    total_list = []
    delta_list = []
    for head_index in range(head_count):
        first = head_index * HDIM
        last = first + HDIM
        outcome = head_grads(
            heads_query[:, first:last],
            heads_grad[:, first:last],
            key_joined_all[:, first:last],
            value_joined_all[:, first:last],
            joined_mask,
            step_weight,
            own_width,
        )
        query_parts.append(outcome[0])
        key_parts.append(outcome[1])
        value_parts.append(outcome[2])
        sgrad_list.append(outcome[3])
        weight_list.append(outcome[4])
        total_list.append(outcome[5])
        delta_list.append(outcome[6])
    query_attn = jnp.concatenate(query_parts, axis=1)
    key_own = jnp.concatenate(key_parts, axis=1)
    value_own = jnp.concatenate(value_parts, axis=1)
    key_terms = []
    value_terms = []
    for head_index in range(head_count):
        first = head_index * HDIM
        last = first + HDIM
        key_terms.append(
            downward(sgrad_list[head_index], heads_query[:, first:last]) * HDIM ** (-0.5)
        )
        value_terms.append(downward(weight_list[head_index], heads_grad[:, first:last]))
    key_back, value_back = from_behind(
        (jnp.concatenate(key_terms, axis=1), jnp.concatenate(value_terms, axis=1)), "span", -1
    )
    key_attn = key_own + key_back
    value_attn = value_own + value_back
    query_tokens, key_tokens, value_tokens = (
        lax.all_to_all(
            query_attn.astype(jnp.bfloat16), "sp", split_axis=0, concat_axis=1, tiled=True
        ),
        lax.all_to_all(
            key_attn.astype(jnp.bfloat16), "sp", split_axis=0, concat_axis=1, tiled=True
        ),
        lax.all_to_all(
            value_attn.astype(jnp.bfloat16), "sp", split_axis=0, concat_axis=1, tiled=True
        ),
    )
    query_back, query_gain = norm_backward(query_tokens, q_normal, q_inverse, gain_full[0])
    key_back_rows, key_gain = norm_backward(key_tokens, k_normal, k_inverse, gain_full[1])
    partial_value = jnp.stack([query_gain, key_gain])
    summed = lax.psum(partial_value, ("span", "sp"))
    gain_grad = lax.psum_scatter(summed, "fsdp", scatter_dimension=1, tiled=True)
    return (query_back[None], key_back_rows[None], value_tokens[None], gain_grad)


def solution(mesh):
    placed = (
        P("fsdp", ("span", "sp"), None),
        P("fsdp", ("span", "sp"), None),
        P("fsdp", ("span", "sp"), None),
        P("fsdp", ("span", "sp"), None),
        P(None, "fsdp"),
        P("fsdp", "span"),
        P("fsdp", None),
    )
    return jax.shard_map(
        on_device,
        mesh=mesh,
        in_specs=placed,
        out_specs=(
            P("fsdp", ("span", "sp"), None),
            P("fsdp", ("span", "sp"), None),
            P("fsdp", ("span", "sp"), None),
            P(None, "fsdp"),
        ),
        check_vma=False,
    )
```

profile of v0, /device:TPU:0, one launch (start us, length us, event | category | flops | bytes accessed | tf_op | source)
XLA Modules:
  0.0 1031.0 jit_solution(12937883028764885410)
XLA Ops:
  9.5 4.2 all-to-all-start.2
  18.8 7.4 all-to-all-done.2
  32.1 9.4 all-to-all-done.1
  41.5 4.3 all-to-all-start.3
  46.3 5.9 collective-permute-start
  53.5 6.6 all-to-all-done.3
  60.1 4.2 all-to-all-start
  72.6 12.8 %all-to-all-done = bf16[128,8,384]{2,0,1:T(8,128)(2,1)} async-done(((bf16[128,8,384]{2,0,1:T(8,128)(2,1)}), bf16[128,8,384]{2,0,1:T(8,128)(2,1)}, u32[]{:S(2)}, u32[]{:S(2)}) %all-to-all-start) | async-done | bytes 786464 | tf_op jit(solution)/shard_map/all_to_all | solution.py:78
  90.4 9.0 fusion.9
  99.4 8.6 exponential_reduce_fusion.2
  108.0 5.4 fusion.68
  113.4 5.4 fusion.61
  118.9 20.2 %fusion.6 = (f32[1024]{0:T(1024)S(1)}, f32[1024]{0:T(1024)S(1)}, f32[1024]{0:T(1024)S(1)}, f32[2048,1024]{0,1:T(8,128)}) fusion(f32[1024]{0:T(1024)S(1)} %log_add_fusion.2, f32[1024,2048]{1,0:T(8,128)} %get-tuple-element.37, pred[1024,1024]{1,0:T(32,128)(4,1)S(1)} %broadcast_compare_fusion, pred[]{:T(512)S(6)} %gt.3, f32[2048,1024]{0,1:T(8,128)} %fusion.68, ...), kind=kOutput, calls=%fused_computation.18 | convolution fusion | flops 569373696 | bytes 53239808 | tf_op jit(solution)/shard_map/dot_general | solution.py:33
  139.1 12.5 %multiply_convert_fusion.2 = (bf16[1024,2048]{1,0:T(8,128)(2,1)S(1)}, bf16[1024,2048]{1,0:T(8,128)(2,1)S(1)}, bf16[1024,2048]{1,0:T(8,128)(2,1)S(1)}, bf16[1024,2048]{1,0:T(8,128)(2,1)S(1)}) fusion(f32[1024]{0:T(1024)S(1)} %select_reduce_fusion, f32[1024]{0:T(1024)S(1)} %log_add_fusion.2, f32[1024,2048]{1,0:T(8,128)} %get-tuple-element.37, ...), kind=kLoop, calls=%fused_computation.26 | loop fusion | flops 33554432 | bytes 51400704 | tf_op jit(solution)/shard_map/convert_element_type | solution.py:58
  168.2 4.9 multiply_convert_fusion.1
  185.2 4.3 all-to-all-start.4
  211.6 21.7 %collective-permute-done.2 = f32[1024,384]{1,0:T(8,128)} collective-permute-done((f32[1024,384]{1,0:T(8,128)}, f32[1024,384]{1,0:T(8,128)}, u32[]{:S(2)}, u32[]{:S(2)}) %collective-permute-start.2) | collective-permute-done | bytes 1572896 | tf_op jit(solution)/shard_map/ppermute | solution.py:14
  235.9 5.6 all-to-all-start.5
  244.2 19.0 %collective-permute-done.3 = f32[1024,384]{0,1:T(8,128)} collective-permute-done((f32[1024,384]{0,1:T(8,128)}, f32[1024,384]{0,1:T(8,128)}, u32[]{:S(2)}, u32[]{:S(2)}) %collective-permute-start.3) | collective-permute-done | bytes 1572896 | tf_op jit(solution)/shard_map/ppermute | solution.py:14
  266.1 10.1 all-to-all-done.5
  276.2 4.2 all-to-all-start.6
  288.2 5.7 all-to-all-done.6
  296.2 37.5 %reduce-scatter.4.cloned.1.call-done = f32[1536,2]{1,0:T(8,128)} async-done(((f32[3072,2]{1,0:T(8,128)}), f32[1536,2]{1,0:T(8,128)}) %reduce-scatter.4.cloned.1.call-update) | async-done | bytes 12304
  335.0 688.9 %psum.8 = f32[2,1536]{1,0:T(2,128)} all-reduce(f32[2,1536]{1,0:T(2,128)S(1)} %copy.105), channel_id=1, replica_groups=mesh['span'=16,'sp'=8,'fsdp'=2] {'span','sp'}, use_global_device_ids=true, to_apply=%region_16.17 | all-reduce | flops 3072 | bytes 24576 | tf_op jit(solution)/shard_map/psum | solution.py:154
  (122 shorter events, 98.4 us)
Async XLA Ops:
  9.5 16.7 %all-to-all-start.2 = ((bf16[128,8,384]{0,2,1:T(8,128)(2,1)}), bf16[128,8,384]{0,2,1:T(8,128)(2,1)}, u32[]{:S(2)}, u32[]{:S(2)}) async-start(bf16[128,8,384]{0,2,1:T(8,128)(2,1)} %bitcast.7), calls=%async_computation.2 | async-start | bytes 1572864 | tf_op jit(solution)/shard_map/all_to_all | solution.py:80
  17.2 28.6 %copy-start.5 = (bf16[1,128,3072]{2,1,0:T(8,128)(2,1)S(1)}, bf16[1,128,3072]{2,1,0:T(8,128)(2,1)}, u32[]{:S(2)}) copy-start(bf16[1,128,3072]{2,1,0:T(8,128)(2,1)} %param.7) | copy-start | bytes 2359300
  26.2 15.2 %all-to-all-start.1 = ((bf16[128,8,384]{2,0,1:T(8,128)(2,1)}), bf16[128,8,384]{2,0,1:T(8,128)(2,1)S(1)}, u32[]{:S(2)}, u32[]{:S(2)}) async-start(bf16[128,8,384]{2,0,1:T(8,128)(2,1)} %multiply_convert_fusion.5), calls=%async_computation.1 | async-start | bytes 1572864 | tf_op jit(solution)/shard_map/all_to_all | solution.py:79
  41.5 22.9 %copy-start.20 = (s32[1,32]{1,0:T(1,128)S(1)}, s32[1,32]{1,0:T(1,128)}, u32[]{:S(2)}) copy-start(s32[1,32]{1,0:T(1,128)} %param.13) | copy-start | bytes 388
  41.5 22.9 %copy-start.19 = (s32[1,1024]{1,0:T(1,128)S(1)}, s32[1,1024]{1,0:T(1,128)}, u32[]{:S(2)}) copy-start(s32[1,1024]{1,0:T(1,128)} %param.12) | copy-start | bytes 12292
  41.5 18.7 %all-to-all-start.3 = ((bf16[128,8,384]{0,2,1:T(8,128)(2,1)}), bf16[128,8,384]{0,2,1:T(8,128)(2,1)}, u32[]{:S(2)}, u32[]{:S(2)}) async-start(bf16[128,8,384]{0,2,1:T(8,128)(2,1)} %bitcast.118), calls=%async_computation.3 | async-start | bytes 1572864 | tf_op jit(solution)/shard_map/all_to_all | solution.py:81
  46.3 39.1 %collective-permute-start = (bf16[1024,384]{1,0:T(8,128)(2,1)S(1)}, bf16[1024,384]{1,0:T(8,128)(2,1)}, u32[]{:S(2)}, u32[]{:S(2)}) collective-permute-start(bf16[1024,384]{1,0:T(8,128)(2,1)S(1)} %bitcast.91), channel_id=1, source_target_pairs={{0,16},{16,32},{32,48},{48,64},{64,80},{80,96},{96,112},{112,128},... | collective-permute-start | bytes 2359304 | tf_op jit(solution)/shard_map/ppermute | solution.py:14
  60.1 25.3 %all-to-all-start = ((bf16[128,8,384]{2,0,1:T(8,128)(2,1)}), bf16[128,8,384]{2,0,1:T(8,128)(2,1)}, u32[]{:S(2)}, u32[]{:S(2)}) async-start(bf16[128,8,384]{2,0,1:T(8,128)(2,1)} %multiply_convert_fusion.6), calls=%async_computation | async-start | bytes 1572864 | tf_op jit(solution)/shard_map/all_to_all | solution.py:78
  69.7 38.3 %collective-permute-start.1 = (bf16[1024,384]{1,0:T(8,128)(2,1)}, bf16[1024,384]{1,0:T(8,128)(2,1)}, u32[]{:S(2)}, u32[]{:S(2)}) collective-permute-start(bf16[1024,384]{1,0:T(8,128)(2,1)} %bitcast.102), channel_id=1, source_target_pairs={{0,16},{16,32},{32,48},{48,64},{64,80},{80,96},{96,112},{112,128},... | collective-permute-start | bytes 2359304 | tf_op jit(solution)/shard_map/ppermute | solution.py:14
  87.7 11.7 %copy-start.1 = (f32[1024,2048]{1,0:T(8,128)}, f32[1024,2048]{1,0:T(8,128)S(1)}, u32[]{:S(2)}) copy-start(f32[1024,2048]{1,0:T(8,128)S(1)} %fusion.75) | copy-start | bytes 25165828
  139.1 12.6 %copy-start.14 = (bf16[8,128,384]{2,1,0:T(8,128)(2,1)S(1)}, bf16[8,128,384]{2,1,0:T(8,128)(2,1)}, u32[]{:S(2)}) copy-start(bf16[8,128,384]{2,1,0:T(8,128)(2,1)} %copy.81) | copy-start | bytes 2359300
  153.3 14.8 %slice-start.2 = ((s8[8388608]{0:T(1024)(128)(4,1)}), s8[4194304]{0:T(1024)(128)(4,1)S(1)}, s32[]{:S(2)}) async-start(s8[8388608]{0:T(1024)(128)(4,1)} %bitcast.89), calls=%async_computation.11 | async-start | bytes 8388608
  155.9 12.2 %slice-start = ((s8[8388608]{0:T(1024)(128)(4,1)}), s8[4194304]{0:T(1024)(128)(4,1)S(1)}, s32[]{:S(2)}) async-start(s8[8388608]{0:T(1024)(128)(4,1)} %bitcast.87), calls=%async_computation.9 | async-start | bytes 8388608
  157.2 10.9 %slice-start.3 = ((s8[8388608]{0:T(1024)(128)(4,1)}), s8[4194304]{0:T(1024)(128)(4,1)S(1)}, s32[]{:S(2)}) async-start(s8[8388608]{0:T(1024)(128)(4,1)} %bitcast.89), calls=%async_computation.12 | async-start | bytes 8388608
  185.2 10.5 %copy-start.18 = (f32[1024,128]{0,1:T(8,128)S(1)}, f32[1024,128]{0,1:T(8,128)}, u32[]{:S(2)}) copy-start(f32[1024,128]{0,1:T(8,128)} %fusion.12) | copy-start | bytes 1572868
  185.2 18.3 %all-to-all-start.4 = ((bf16[8,128,384]{2,1,0:T(8,128)(2,1)}), bf16[8,128,384]{2,1,0:T(8,128)(2,1)}, u32[]{:S(2)}, u32[]{:S(2)}) async-start(bf16[8,128,384]{2,1,0:T(8,128)(2,1)} %pad_maximum_fusion.2), calls=%async_computation.4 | async-start | bytes 1572864 | tf_op jit(solution)/shard_map/all_to_all | solution.py:141
  192.4 41.0 %collective-permute-start.2 = (f32[1024,384]{1,0:T(8,128)}, f32[1024,384]{1,0:T(8,128)}, u32[]{:S(2)}, u32[]{:S(2)}) collective-permute-start(f32[1024,384]{1,0:T(8,128)} %pad_maximum_fusion), channel_id=1, source_target_pairs={{16,0},{32,16},{48,32},{64,48},{80,64},{96,80},{112,96},{128,112},... | collective-permute-start | bytes 4718600 | tf_op jit(solution)/shard_map/ppermute | solution.py:14
  197.0 66.2 %collective-permute-start.3 = (f32[1024,384]{0,1:T(8,128)}, f32[1024,384]{0,1:T(8,128)}, u32[]{:S(2)}, u32[]{:S(2)}) collective-permute-start(f32[1024,384]{0,1:T(8,128)} %pad_maximum_fusion.1), channel_id=1, source_target_pairs={{16,0},{32,16},{48,32},{64,48},{80,64},{96,80},{112,96},{128,112},... | collective-permute-start | bytes 4718600 | tf_op jit(solution)/shard_map/ppermute | solution.py:14
  205.6 27.8 %copy-start.15 = (f32[1024,128]{1,0:T(8,128)S(1)}, f32[1024,128]{1,0:T(8,128)}, u32[]{:S(2)}) copy-start(f32[1024,128]{1,0:T(8,128)} %fusion.38) | copy-start | bytes 1572868
  205.6 27.7 %copy-start.16 = (f32[1024,128]{1,0:T(8,128)S(1)}, f32[1024,128]{1,0:T(8,128)}, u32[]{:S(2)}) copy-start(f32[1024,128]{1,0:T(8,128)} %fusion.44) | copy-start | bytes 1572868
  209.0 32.5 %copy-start.6 = (bf16[1,128,3072]{2,1,0:T(8,128)(2,1)S(1)}, bf16[1,128,3072]{2,1,0:T(8,128)(2,1)}, u32[]{:S(2)}) copy-start(bf16[1,128,3072]{2,1,0:T(8,128)(2,1)} %param.7) | copy-start | bytes 2359300
  235.9 40.3 %all-to-all-start.5 = ((bf16[8,128,384]{2,1,0:T(8,128)(2,1)}), bf16[8,128,384]{2,1,0:T(8,128)(2,1)S(1)}, u32[]{:S(2)}, u32[]{:S(2)}) async-start(bf16[8,128,384]{2,1,0:T(8,128)(2,1)} %bitcast.119), calls=%async_computation.5 | async-start | bytes 1572864 | tf_op jit(solution)/shard_map/all_to_all | solution.py:144
  276.2 17.6 %all-to-all-start.6 = ((bf16[8,128,384]{1,2,0:T(8,128)(2,1)}), bf16[8,128,384]{1,2,0:T(8,128)(2,1)}, u32[]{:S(2)}, u32[]{:S(2)}) async-start(bf16[8,128,384]{1,2,0:T(8,128)(2,1)} %copy_bitcast_fusion), calls=%async_computation.6 | async-start | bytes 1572864 | tf_op jit(solution)/shard_map/all_to_all | solution.py:147
  280.5 53.2 %reduce-scatter.4.cloned.1.call-start = ((), (), s32[]{:S(2)}) async-start(), calls=%async_computation.8 | async-start | bytes 2359296
  (13 other events, 95.5 us)
Sparse Core Ops, SparseCore 0:
  287.0 46.5 reduce-scatter.3
where the time goes:
time: 1040 us; the launch traced here: 1030 us
  blocking collectives  691 us (66%)
  waiting for transfers between devices  130 us (12%)
  matrix products  79.4 us (8%)
  other arithmetic  48.8 us (5%)
  starting transfers between devices  42.3 us (4%)
  local copies, waits for them, and re-layouts  24.5 us (2%)
  between operations  14.8 us (1%)
    psum x1, blocking collectives, on_device(): summed = lax.psum(partial_value, ('span', 'sp'))  689 us
    dot_general x6, matrix products, across(): lax.dot_general(left, right, (((1,), (1,)), ((), ())), preferred_element_...  45 us
    ppermute x4, waiting for transfers between devices, from_behind(): lax.ppermute(value, axis, [(source, source + steps) for source in range(f...  40.7 us
    unnamed x2, waiting for transfers between devices  37.5 us
    dot_general x12, matrix products, downward(): lax.dot_general(left, right, (((0,), (0,)), ((), ())), preferred_element_...  26.4 us
  transfers between devices with their start and end apart: 12, of which 9 were waited for; matrix products, arithmetic and copies ran while one was open for 7% of the time, Pallas kernels for 0%

commit v1 on v0

--- a/solution.py
+++ b/solution.py
@@ -151,7 +151,7 @@
     query_back, query_gain = norm_backward(query_tokens, q_normal, q_inverse, gain_full[0])
     key_back_rows, key_gain = norm_backward(key_tokens, k_normal, k_inverse, gain_full[1])
     partial_value = jnp.stack([query_gain, key_gain])
-    summed = lax.psum(partial_value, ("span", "sp"))
+    summed = lax.psum(lax.psum(partial_value, "sp"), "span")
     gain_grad = lax.psum_scatter(summed, "fsdp", scatter_dimension=1, tiled=True)
     return (query_back[None], key_back_rows[None], value_tokens[None], gain_grad)
 

time: 1040 us -> 460 us (0.44)
  blocking collectives: 691 us -> 113 us
    psum x1 -> x2, blocking collectives: 689 us -> 111 us  [on_device(): summed = lax.psum(lax.psum(partial_value, 'sp'), 'span')]
  transfers between devices with their start and end apart: 12 -> 12, of which waited for: 9 -> 9; matrix products, arithmetic and copies ran while one was open for 7% -> 16% of each run, Pallas kernels for 0% -> 0%
where the time goes in v1:
time: 460 us; the launch traced here: 453 us
  waiting for transfers between devices  130 us (28%)
  blocking collectives  113 us (25%)
  matrix products  79.4 us (17%)
  other arithmetic  48.8 us (11%)
  starting transfers between devices  42.3 us (9%)
  local copies, waits for them, and re-layouts  24.5 us (5%)
  between operations  14.8 us (3%)
    psum x2, blocking collectives, on_device(): summed = lax.psum(lax.psum(partial_value, 'sp'), 'span')  111 us
    dot_general x6, matrix products, across(): lax.dot_general(left, right, (((1,), (1,)), ((), ())), preferred_element_...  45 us
    ppermute x4, waiting for transfers between devices, from_behind(): lax.ppermute(value, axis, [(source, source + steps) for source in range(f...  40.7 us
    unnamed x2, waiting for transfers between devices  37.5 us
    dot_general x12, matrix products, downward(): lax.dot_general(left, right, (((0,), (0,)), ((), ())), preferred_element_...  26.4 us
    convert_element_type x2, other arithmetic, head_grads(): weights = (factor * probs).astype(jnp.bfloat16)  17.4 us
    all_to_all x1, waiting for transfers between devices, on_device(): lax.all_to_all(q_ready, 'sp', split_axis=1, concat_axis=0, tiled=True)  12.8 us
    ppermute x4, starting transfers between devices, from_behind(): lax.ppermute(value, axis, [(source, source + steps) for source in range(f...  11.8 us
  transfers between devices with their start and end apart: 12, of which 9 were waited for; matrix products, arithmetic and copies ran while one was open for 16% of the time, Pallas kernels for 0%

profile of v1, /device:TPU:0, one launch (start us, length us, event | category | flops | bytes accessed | tf_op | source)
XLA Modules:
  0.0 453.3 jit_solution(6179762665885015336)
XLA Ops:
  18.8 7.4 %all-to-all-done.2 = bf16[128,8,384]{0,2,1:T(8,128)(2,1)} async-done(((bf16[128,8,384]{0,2,1:T(8,128)(2,1)}), bf16[128,8,384]{0,2,1:T(8,128)(2,1)}, u32[]{:S(2)}, u32[]{:S(2)}) %all-to-all-start.2) | async-done | bytes 786464 | tf_op jit(solution)/shard_map/all_to_all | solution.py:80
  32.1 9.4 %all-to-all-done.1 = bf16[128,8,384]{2,0,1:T(8,128)(2,1)S(1)} async-done(((bf16[128,8,384]{2,0,1:T(8,128)(2,1)}), bf16[128,8,384]{2,0,1:T(8,128)(2,1)S(1)}, u32[]{:S(2)}, u32[]{:S(2)}) %all-to-all-start.1) | async-done | bytes 786464 | tf_op jit(solution)/shard_map/all_to_all | solution.py:79
  41.5 4.3 all-to-all-start.3
  46.3 5.9 %collective-permute-start = (bf16[1024,384]{1,0:T(8,128)(2,1)S(1)}, bf16[1024,384]{1,0:T(8,128)(2,1)}, u32[]{:S(2)}, u32[]{:S(2)}) collective-permute-start(bf16[1024,384]{1,0:T(8,128)(2,1)S(1)} %bitcast.91), channel_id=1, source_target_pairs={{0,16},{16,32},{32,48},{48,64},{64,80},{80,96},{96,112},{112,128},... | collective-permute-start | bytes 2359304 | tf_op jit(solution)/shard_map/ppermute | solution.py:14
  53.5 6.6 %all-to-all-done.3 = bf16[128,8,384]{0,2,1:T(8,128)(2,1)} async-done(((bf16[128,8,384]{0,2,1:T(8,128)(2,1)}), bf16[128,8,384]{0,2,1:T(8,128)(2,1)}, u32[]{:S(2)}, u32[]{:S(2)}) %all-to-all-start.3) | async-done | bytes 786464 | tf_op jit(solution)/shard_map/all_to_all | solution.py:81
  60.1 4.2 all-to-all-start
  72.6 12.8 %all-to-all-done = bf16[128,8,384]{2,0,1:T(8,128)(2,1)} async-done(((bf16[128,8,384]{2,0,1:T(8,128)(2,1)}), bf16[128,8,384]{2,0,1:T(8,128)(2,1)}, u32[]{:S(2)}, u32[]{:S(2)}) %all-to-all-start) | async-done | bytes 786464 | tf_op jit(solution)/shard_map/all_to_all | solution.py:78
  90.4 9.0 %fusion.9 = (f32[1024]{0:T(1024)S(1)}, f32[1024]{0:T(1024)S(1)}, f32[1024]{0:T(1024)S(1)}, f32[1024,2048]{1,0:T(8,128)}) fusion(pred[1024,1024]{1,0:T(32,128)(4,1)S(1)} %broadcast_compare_fusion, pred[]{:T(512)S(6)} %gt.3, f32[1024,2048]{1,0:T(8,128)S(1)} %fusion.82, f32[1024,2048]{1,0:T(8,128)S(1)} %fusion.75, bf16[1024,384]{1,0:T(8,128)(2,1)S(1)} %bitcast.94, ...), kind=kOutput, calls=%fused_computation.27 | convolution fusion | flops 556790784 | bytes 28061696 | tf_op jit(solution)/shard_map/dot_general | solution.py:33
  99.4 8.6 %exponential_reduce_fusion.2 = (f32[1024]{0:T(1024)S(1)}, f32[1024]{0:T(1024)S(1)}, f32[1024]{0:T(1024)S(1)}) fusion(f32[1024,2048]{1,0:T(8,128)} %get-tuple-element.37, pred[1024,1024]{1,0:T(32,128)(4,1)S(1)} %broadcast_compare_fusion, pred[]{:T(512)S(6)} %gt.3, f32[1024]{0:T(1024)S(1)} %get-tuple-element.22, f32[1024]{0:T(1024)S(1)} %get-tuple-element.24, ...), kind=kLoop, calls=%fused_computation.23 | loop fusion | flops 25162752 | bytes 26238976 | tf_op jit(solution)/shard_map/reduce_sum | solution.py:51
  108.0 5.4 %fusion.68 = f32[2048,1024]{0,1:T(8,128)} fusion(bf16[1024,384]{1,0:T(8,128)(2,1)} %collective-permute-done.1, bf16[1024,384]{1,0:T(8,128)(2,1)S(1)} %bitcast.104, bf16[1024,384]{1,0:T(8,128)(2,1)S(1)} %bitcast.112), kind=kOutput, calls=%fused_computation.105 | convolution fusion | flops 537919488 | bytes 10223616 | tf_op jit(solution)/shard_map/dot_general | solution.py:33
  113.4 5.4 %fusion.61 = f32[2048,1024]{0,1:T(8,128)} fusion(bf16[1024,384]{1,0:T(8,128)(2,1)S(1)} %bitcast.105, bf16[1024,384]{1,0:T(8,128)(2,1)} %collective-permute-done.1, bf16[1024,384]{1,0:T(8,128)(2,1)S(1)} %bitcast.113), kind=kOutput, calls=%fused_computation.99 | convolution fusion | flops 537919488 | bytes 10223616 | tf_op jit(solution)/shard_map/dot_general | solution.py:33
  118.9 20.2 %fusion.6 = (f32[1024]{0:T(1024)S(1)}, f32[1024]{0:T(1024)S(1)}, f32[1024]{0:T(1024)S(1)}, f32[2048,1024]{0,1:T(8,128)}) fusion(f32[1024]{0:T(1024)S(1)} %log_add_fusion.2, f32[1024,2048]{1,0:T(8,128)} %get-tuple-element.37, pred[1024,1024]{1,0:T(32,128)(4,1)S(1)} %broadcast_compare_fusion, pred[]{:T(512)S(6)} %gt.3, f32[2048,1024]{0,1:T(8,128)} %fusion.68, ...), kind=kOutput, calls=%fused_computation.18 | convolution fusion | flops 569373696 | bytes 53239808 | tf_op jit(solution)/shard_map/dot_general | solution.py:33
  139.1 12.5 %multiply_convert_fusion.2 = (bf16[1024,2048]{1,0:T(8,128)(2,1)S(1)}, bf16[1024,2048]{1,0:T(8,128)(2,1)S(1)}, bf16[1024,2048]{1,0:T(8,128)(2,1)S(1)}, bf16[1024,2048]{1,0:T(8,128)(2,1)S(1)}) fusion(f32[1024]{0:T(1024)S(1)} %select_reduce_fusion, f32[1024]{0:T(1024)S(1)} %log_add_fusion.2, f32[1024,2048]{1,0:T(8,128)} %get-tuple-element.37, ...), kind=kLoop, calls=%fused_computation.26 | loop fusion | flops 33554432 | bytes 51400704 | tf_op jit(solution)/shard_map/convert_element_type | solution.py:58
  168.2 4.9 %multiply_convert_fusion.1 = (bf16[1024,2048]{1,0:T(8,128)(2,1)}, bf16[1024,2048]{1,0:T(8,128)(2,1)}) fusion(f32[1024]{0:T(1024)S(1)} %select_reduce_fusion, f32[1024]{0:T(1024)S(1)} %get-tuple-element.40, f32[1024,2048]{1,0:T(8,128)S(1)} %bitcast.88, pred[1024,1024]{1,0:T(32,128)(4,1)S(1)} %broadcast_compare_fusion, pred[]{:T(512)S(6)} %gt.3, ...), kind=kLoop, calls=%fused_computation.25 | loop fusion | flops 16777216 | bytes 26226688 | tf_op jit(solution)/shard_map/convert_element_type | solution.py:58
  185.2 4.3 all-to-all-start.4
  211.6 21.7 %collective-permute-done.2 = f32[1024,384]{1,0:T(8,128)} collective-permute-done((f32[1024,384]{1,0:T(8,128)}, f32[1024,384]{1,0:T(8,128)}, u32[]{:S(2)}, u32[]{:S(2)}) %collective-permute-start.2) | collective-permute-done | bytes 1572896 | tf_op jit(solution)/shard_map/ppermute | solution.py:14
  235.9 5.6 %all-to-all-start.5 = ((bf16[8,128,384]{2,1,0:T(8,128)(2,1)}), bf16[8,128,384]{2,1,0:T(8,128)(2,1)S(1)}, u32[]{:S(2)}, u32[]{:S(2)}) async-start(bf16[8,128,384]{2,1,0:T(8,128)(2,1)} %bitcast.119), calls=%async_computation.5 | async-start | bytes 1572864 | tf_op jit(solution)/shard_map/all_to_all | solution.py:144
  244.2 19.0 %collective-permute-done.3 = f32[1024,384]{0,1:T(8,128)} collective-permute-done((f32[1024,384]{0,1:T(8,128)}, f32[1024,384]{0,1:T(8,128)}, u32[]{:S(2)}, u32[]{:S(2)}) %collective-permute-start.3) | collective-permute-done | bytes 1572896 | tf_op jit(solution)/shard_map/ppermute | solution.py:14
  266.1 10.1 %all-to-all-done.5 = bf16[8,128,384]{2,1,0:T(8,128)(2,1)S(1)} async-done(((bf16[8,128,384]{2,1,0:T(8,128)(2,1)}), bf16[8,128,384]{2,1,0:T(8,128)(2,1)S(1)}, u32[]{:S(2)}, u32[]{:S(2)}) %all-to-all-start.5) | async-done | bytes 786464 | tf_op jit(solution)/shard_map/all_to_all | solution.py:144
  276.2 4.2 all-to-all-start.6
  288.2 5.7 %all-to-all-done.6 = bf16[8,128,384]{1,2,0:T(8,128)(2,1)} async-done(((bf16[8,128,384]{1,2,0:T(8,128)(2,1)}), bf16[8,128,384]{1,2,0:T(8,128)(2,1)}, u32[]{:S(2)}, u32[]{:S(2)}) %all-to-all-start.6) | async-done | bytes 786464 | tf_op jit(solution)/shard_map/all_to_all | solution.py:147
  296.2 37.5 %reduce-scatter.4.cloned.1.call-done = f32[1536,2]{1,0:T(8,128)} async-done(((f32[3072,2]{1,0:T(8,128)}), f32[1536,2]{1,0:T(8,128)}) %reduce-scatter.4.cloned.1.call-update) | async-done | bytes 12304
  335.0 34.0 %psum.17 = f32[2,1536]{1,0:T(2,128)S(1)} all-reduce(f32[2,1536]{1,0:T(2,128)S(1)} %copy.105), channel_id=1, replica_groups=mesh['span'=16,'sp'=8,'fsdp'=2] {'sp'}, use_global_device_ids=true, to_apply=%region_16.17 | all-reduce | flops 3072 | bytes 24576 | tf_op jit(solution)/shard_map/psum | solution.py:154
  369.1 77.2 %psum.16 = f32[2,1536]{1,0:T(2,128)} all-reduce(f32[2,1536]{1,0:T(2,128)S(1)} %psum.17), channel_id=1, replica_groups=mesh['span'=16,'sp'=8,'fsdp'=2] {'span'}, use_global_device_ids=true, to_apply=%region_17.18 | all-reduce | flops 3072 | bytes 24576 | tf_op jit(solution)/shard_map/psum | solution.py:154
  (123 shorter events, 102.6 us)
Async XLA Ops:
  9.5 16.7 %all-to-all-start.2 = ((bf16[128,8,384]{0,2,1:T(8,128)(2,1)}), bf16[128,8,384]{0,2,1:T(8,128)(2,1)}, u32[]{:S(2)}, u32[]{:S(2)}) async-start(bf16[128,8,384]{0,2,1:T(8,128)(2,1)} %bitcast.7), calls=%async_computation.2 | async-start | bytes 1572864 | tf_op jit(solution)/shard_map/all_to_all | solution.py:80
  17.2 28.6 %copy-start.5 = (bf16[1,128,3072]{2,1,0:T(8,128)(2,1)S(1)}, bf16[1,128,3072]{2,1,0:T(8,128)(2,1)}, u32[]{:S(2)}) copy-start(bf16[1,128,3072]{2,1,0:T(8,128)(2,1)} %param.7) | copy-start | bytes 2359300
  26.2 15.2 %all-to-all-start.1 = ((bf16[128,8,384]{2,0,1:T(8,128)(2,1)}), bf16[128,8,384]{2,0,1:T(8,128)(2,1)S(1)}, u32[]{:S(2)}, u32[]{:S(2)}) async-start(bf16[128,8,384]{2,0,1:T(8,128)(2,1)} %multiply_convert_fusion.5), calls=%async_computation.1 | async-start | bytes 1572864 | tf_op jit(solution)/shard_map/all_to_all | solution.py:79
  41.5 22.9 %copy-start.20 = (s32[1,32]{1,0:T(1,128)S(1)}, s32[1,32]{1,0:T(1,128)}, u32[]{:S(2)}) copy-start(s32[1,32]{1,0:T(1,128)} %param.13) | copy-start | bytes 388
  41.5 22.9 %copy-start.19 = (s32[1,1024]{1,0:T(1,128)S(1)}, s32[1,1024]{1,0:T(1,128)}, u32[]{:S(2)}) copy-start(s32[1,1024]{1,0:T(1,128)} %param.12) | copy-start | bytes 12292
  41.5 18.7 %all-to-all-start.3 = ((bf16[128,8,384]{0,2,1:T(8,128)(2,1)}), bf16[128,8,384]{0,2,1:T(8,128)(2,1)}, u32[]{:S(2)}, u32[]{:S(2)}) async-start(bf16[128,8,384]{0,2,1:T(8,128)(2,1)} %bitcast.118), calls=%async_computation.3 | async-start | bytes 1572864 | tf_op jit(solution)/shard_map/all_to_all | solution.py:81
  46.3 39.1 %collective-permute-start = (bf16[1024,384]{1,0:T(8,128)(2,1)S(1)}, bf16[1024,384]{1,0:T(8,128)(2,1)}, u32[]{:S(2)}, u32[]{:S(2)}) collective-permute-start(bf16[1024,384]{1,0:T(8,128)(2,1)S(1)} %bitcast.91), channel_id=1, source_target_pairs={{0,16},{16,32},{32,48},{48,64},{64,80},{80,96},{96,112},{112,128},... | collective-permute-start | bytes 2359304 | tf_op jit(solution)/shard_map/ppermute | solution.py:14
  60.1 25.3 %all-to-all-start = ((bf16[128,8,384]{2,0,1:T(8,128)(2,1)}), bf16[128,8,384]{2,0,1:T(8,128)(2,1)}, u32[]{:S(2)}, u32[]{:S(2)}) async-start(bf16[128,8,384]{2,0,1:T(8,128)(2,1)} %multiply_convert_fusion.6), calls=%async_computation | async-start | bytes 1572864 | tf_op jit(solution)/shard_map/all_to_all | solution.py:78
  69.7 38.3 %collective-permute-start.1 = (bf16[1024,384]{1,0:T(8,128)(2,1)}, bf16[1024,384]{1,0:T(8,128)(2,1)}, u32[]{:S(2)}, u32[]{:S(2)}) collective-permute-start(bf16[1024,384]{1,0:T(8,128)(2,1)} %bitcast.102), channel_id=1, source_target_pairs={{0,16},{16,32},{32,48},{48,64},{64,80},{80,96},{96,112},{112,128},... | collective-permute-start | bytes 2359304 | tf_op jit(solution)/shard_map/ppermute | solution.py:14
  87.7 11.7 %copy-start.1 = (f32[1024,2048]{1,0:T(8,128)}, f32[1024,2048]{1,0:T(8,128)S(1)}, u32[]{:S(2)}) copy-start(f32[1024,2048]{1,0:T(8,128)S(1)} %fusion.75) | copy-start | bytes 25165828
  139.1 12.6 %copy-start.14 = (bf16[8,128,384]{2,1,0:T(8,128)(2,1)S(1)}, bf16[8,128,384]{2,1,0:T(8,128)(2,1)}, u32[]{:S(2)}) copy-start(bf16[8,128,384]{2,1,0:T(8,128)(2,1)} %copy.81) | copy-start | bytes 2359300
  153.3 14.8 %slice-start.2 = ((s8[8388608]{0:T(1024)(128)(4,1)}), s8[4194304]{0:T(1024)(128)(4,1)S(1)}, s32[]{:S(2)}) async-start(s8[8388608]{0:T(1024)(128)(4,1)} %bitcast.89), calls=%async_computation.11 | async-start | bytes 8388608
  155.9 12.2 %slice-start = ((s8[8388608]{0:T(1024)(128)(4,1)}), s8[4194304]{0:T(1024)(128)(4,1)S(1)}, s32[]{:S(2)}) async-start(s8[8388608]{0:T(1024)(128)(4,1)} %bitcast.87), calls=%async_computation.9 | async-start | bytes 8388608
  157.2 10.9 %slice-start.3 = ((s8[8388608]{0:T(1024)(128)(4,1)}), s8[4194304]{0:T(1024)(128)(4,1)S(1)}, s32[]{:S(2)}) async-start(s8[8388608]{0:T(1024)(128)(4,1)} %bitcast.89), calls=%async_computation.12 | async-start | bytes 8388608
  185.2 10.5 %copy-start.18 = (f32[1024,128]{0,1:T(8,128)S(1)}, f32[1024,128]{0,1:T(8,128)}, u32[]{:S(2)}) copy-start(f32[1024,128]{0,1:T(8,128)} %fusion.12) | copy-start | bytes 1572868
  185.2 18.3 %all-to-all-start.4 = ((bf16[8,128,384]{2,1,0:T(8,128)(2,1)}), bf16[8,128,384]{2,1,0:T(8,128)(2,1)}, u32[]{:S(2)}, u32[]{:S(2)}) async-start(bf16[8,128,384]{2,1,0:T(8,128)(2,1)} %pad_maximum_fusion.2), calls=%async_computation.4 | async-start | bytes 1572864 | tf_op jit(solution)/shard_map/all_to_all | solution.py:141
  192.4 41.0 %collective-permute-start.2 = (f32[1024,384]{1,0:T(8,128)}, f32[1024,384]{1,0:T(8,128)}, u32[]{:S(2)}, u32[]{:S(2)}) collective-permute-start(f32[1024,384]{1,0:T(8,128)} %pad_maximum_fusion), channel_id=1, source_target_pairs={{16,0},{32,16},{48,32},{64,48},{80,64},{96,80},{112,96},{128,112},... | collective-permute-start | bytes 4718600 | tf_op jit(solution)/shard_map/ppermute | solution.py:14
  197.0 66.2 %collective-permute-start.3 = (f32[1024,384]{0,1:T(8,128)}, f32[1024,384]{0,1:T(8,128)}, u32[]{:S(2)}, u32[]{:S(2)}) collective-permute-start(f32[1024,384]{0,1:T(8,128)} %pad_maximum_fusion.1), channel_id=1, source_target_pairs={{16,0},{32,16},{48,32},{64,48},{80,64},{96,80},{112,96},{128,112},... | collective-permute-start | bytes 4718600 | tf_op jit(solution)/shard_map/ppermute | solution.py:14
  205.6 27.8 %copy-start.15 = (f32[1024,128]{1,0:T(8,128)S(1)}, f32[1024,128]{1,0:T(8,128)}, u32[]{:S(2)}) copy-start(f32[1024,128]{1,0:T(8,128)} %fusion.38) | copy-start | bytes 1572868
  205.6 27.7 %copy-start.16 = (f32[1024,128]{1,0:T(8,128)S(1)}, f32[1024,128]{1,0:T(8,128)}, u32[]{:S(2)}) copy-start(f32[1024,128]{1,0:T(8,128)} %fusion.44) | copy-start | bytes 1572868
  209.0 32.5 %copy-start.6 = (bf16[1,128,3072]{2,1,0:T(8,128)(2,1)S(1)}, bf16[1,128,3072]{2,1,0:T(8,128)(2,1)}, u32[]{:S(2)}) copy-start(bf16[1,128,3072]{2,1,0:T(8,128)(2,1)} %param.7) | copy-start | bytes 2359300
  235.9 40.3 %all-to-all-start.5 = ((bf16[8,128,384]{2,1,0:T(8,128)(2,1)}), bf16[8,128,384]{2,1,0:T(8,128)(2,1)S(1)}, u32[]{:S(2)}, u32[]{:S(2)}) async-start(bf16[8,128,384]{2,1,0:T(8,128)(2,1)} %bitcast.119), calls=%async_computation.5 | async-start | bytes 1572864 | tf_op jit(solution)/shard_map/all_to_all | solution.py:144
  276.2 17.6 %all-to-all-start.6 = ((bf16[8,128,384]{1,2,0:T(8,128)(2,1)}), bf16[8,128,384]{1,2,0:T(8,128)(2,1)}, u32[]{:S(2)}, u32[]{:S(2)}) async-start(bf16[8,128,384]{1,2,0:T(8,128)(2,1)} %copy_bitcast_fusion), calls=%async_computation.6 | async-start | bytes 1572864 | tf_op jit(solution)/shard_map/all_to_all | solution.py:147
  280.5 53.2 %reduce-scatter.4.cloned.1.call-start = ((), (), s32[]{:S(2)}) async-start(), calls=%async_computation.8 | async-start | bytes 2359296
  (13 other events, 95.5 us)
Sparse Core Ops, SparseCore 0:
  287.0 46.5 reduce-scatter.3
